TPU v7x, 128 devices: a whole 4x4x4 slice. The times are simulated.
128 devices in a mesh: side: 2 (over core), grp: 8 (over x_hi, y), tp: 8 (over x_lo, z).
Axes of the slice: x: 4 (x_hi: 2, x_lo: 2; x = x_hi * 2 + x_lo), y: 4, z: 4, core: 2. Of those that a mesh axis runs over, the one named last changes fastest.
Arguments:
- queries: bfloat16 [192, 4096], P('grp', 'side'), may hold values from -6 to 6
- kv_cache: bfloat16 [192, 16, 192, 256], P('grp', ('side', 'tp')), may hold values from -6 to 6
- lengths: int32 [192], P('grp'), may hold values from 2 to 768, as said below
- out_weight: bfloat16 [4096, 2048], P(('side', 'tp')), may hold values from -1 to 1
- resid: bfloat16 [192, 2048], P('grp'), may hold values from -6 to 6
- norm_gain: float32 [2048], replicated, may hold values from 0.1 to 1.9
- expert_ids: int32 [192, 8], P('grp'), may hold values from 0 to 127, all different within a row; in each aligned block of 24 rows (0 to 23, 24 to 47, ...) at most 3 rows name the same one
- expert_gates: float32 [192, 8], P('grp'), may hold values from 0.05 to 1
- w_gate_up: bfloat16 [128, 2048, 1536], P(('side', 'grp', 'tp')), may hold values from -0.125 to 0.125
- w_down: bfloat16 [128, 768, 2048], P(('side', 'grp', 'tp')), may hold values from -0.21875 to 0.21875
Outputs:
- layer_out: bfloat16 [192, 2048], P('grp', ('side', 'tp'))
Inputs may be any that keep to these rules, and one draw needn't show every extreme that they name: `lengths`: every row's cache holds at least two tokens; some row holds exactly 768. `expert_ids`: each row names 8 different experts. Among the rows of one row group no expert is named by more than 3 rows; in some group an expert is named by exactly 3.
All inputs are finite; a program needn't handle non-finite values.
Results may differ from a plain program's by a relative error of at most 0.017.
Values may be sent and summed in bfloat16 or wider, within the bound.
A program may use at most 64 MiB of HBM per device.

v0:
```python
import math
import jax
import jax.numpy as jnp
from jax import lax
from jax.sharding import PartitionSpec as P

QH = 32
KVH = 4
HD = 128
TOPK = 8


def swapped(value, axis, distance):
    mask = 2**distance
    pairs = [(source, source ^ mask) for source in range(lax.axis_size(axis))]
    return lax.ppermute(value, axis, pairs)


def body(
    queries,
    kv_cache,
    lengths,
    out_weight,
    resid,
    norm_gain,
    expert_ids,
    expert_gates,
    w_gate_up,
    w_down,
):
    lane_count = lax.axis_size("tp")
    tp_index = lax.axis_index("tp")
    side_count = lax.axis_size("side")
    section = lax.axis_index("side")
    grp_count = lax.axis_size("grp")
    group_size = side_count * lane_count
    member_index = section * lane_count + tp_index
    kv_parts = group_size // KVH
    group_heads = QH // KVH
    per_member = QH // group_size
    part_span = kv_cache.shape[2]
    model_width = out_weight.shape[1]
    piece_width = model_width // group_size
    rows_grp = lengths.shape[0]
    local_experts = w_gate_up.shape[0]
    experts_all = local_experts * side_count * grp_count * lane_count
    capacity = max(2, 2 * rows_grp * TOPK // experts_all)
    head_start = tp_index // kv_parts * group_heads * HD
    part_index = tp_index % kv_parts
    row_count = queries.shape[0]
    query_rows = lax.dynamic_slice_in_dim(queries, head_start, group_heads * HD, 1).reshape(
        row_count, group_heads, HD
    )
    key_rows = kv_cache[:, 0, :, :HD]
    value_rows = kv_cache[:, 0, :, HD:]
    positions = part_index * part_span + jnp.arange(part_span, dtype=jnp.int32)
    valid_mask = (positions[None, :] < lengths[:, None])[:, None, :]
    scores = jnp.einsum(
        "rgd,rpd->rgp", query_rows, key_rows, preferred_element_type=jnp.float32
    ) / math.sqrt(HD)
    scores = jnp.where(valid_mask, scores, -1e30)
    row_max = jnp.max(scores, axis=-1)
    for bit_index in range(kv_parts.bit_length() - 1):
        row_max = jnp.maximum(row_max, swapped(row_max, "tp", bit_index))
    weights = jnp.where(valid_mask, jnp.exp(scores - row_max[..., None]), 0.0)
    weight_sum = jnp.sum(weights, axis=-1)
    numerator = jnp.einsum(
        "rgp,rpd->rgd", weights.astype(jnp.bfloat16), value_rows, preferred_element_type=jnp.float32
    )
    for bit_index in range(kv_parts.bit_length() - 1):
        other_numerator, other_sum = swapped((numerator, weight_sum), "tp", bit_index)
        numerator = numerator + other_numerator
        weight_sum = weight_sum + other_sum
    heads_out = (numerator / weight_sum[..., None]).astype(jnp.bfloat16)
    mine = lax.dynamic_slice_in_dim(heads_out, part_index * per_member, per_member, 1).reshape(
        row_count, per_member * HD
    )
    projected = jnp.dot(mine, out_weight, preferred_element_type=jnp.float32)
    summed = lax.psum(projected, ("side", "tp"))
    middle = (resid.astype(jnp.float32) + summed).astype(jnp.bfloat16)
    middle_wide = middle.astype(jnp.float32)
    inv_rms = lax.rsqrt(jnp.mean(middle_wide * middle_wide, axis=-1, keepdims=True) + 1e-06)
    normed = (middle_wide * inv_rms * norm_gain).astype(jnp.bfloat16)
    column_experts = (
        (
            (section * grp_count + jnp.arange(grp_count, dtype=jnp.int32)[:, None]) * lane_count
            + tp_index
        )
        * local_experts
        + jnp.arange(local_experts, dtype=jnp.int32)[None, :]
    ).reshape(-1)
    matches = expert_ids[:, :, None] == column_experts[None, None, :]
    hit_count = jnp.sum(matches.astype(jnp.int32), axis=1)
    gate_cols = jnp.sum(jnp.where(matches, expert_gates[:, :, None], 0.0), axis=1)
    slot_rank = jnp.cumsum(hit_count, axis=0) - hit_count
    slot_ids = jnp.arange(capacity, dtype=jnp.int32)
    placed = (hit_count[:, :, None] == 1) & (slot_rank[:, :, None] == slot_ids[None, None, :])
    send_map = placed.astype(jnp.bfloat16)
    outgoing = jnp.einsum(
        "rcs,rd->csd", send_map, normed, preferred_element_type=jnp.float32
    ).astype(jnp.bfloat16)
    outgoing = outgoing.reshape(grp_count, local_experts, capacity, model_width)
    hidden = jnp.einsum(
        "gjcd,jdf->gjcf",
        lax.all_to_all(outgoing, "grp", split_axis=0, concat_axis=0, tiled=True),
        w_gate_up,
        preferred_element_type=jnp.float32,
    )
    inner_width = hidden.shape[-1] // 2
    activated = (jax.nn.silu(hidden[..., :inner_width]) * hidden[..., inner_width:]).astype(
        jnp.bfloat16
    )
    produced = jnp.einsum(
        "gjcf,jfd->gjcd", activated, w_down, preferred_element_type=jnp.float32
    ).astype(jnp.bfloat16)
    returned = lax.all_to_all(produced, "grp", split_axis=0, concat_axis=0, tiled=True)
    combine_weights = (send_map.astype(jnp.float32) * gate_cols[:, :, None]).reshape(row_count, -1)
    moe_part = jnp.dot(
        combine_weights,
        returned.reshape(-1, model_width).astype(jnp.float32),
        precision=lax.Precision.HIGHEST,
    )
    middle_mine = lax.dynamic_slice_in_dim(middle_wide, member_index * piece_width, piece_width, 1)
    moe_whole = lax.psum(moe_part, ("side", "tp"))
    return (
        middle_mine
        + lax.dynamic_slice_in_dim(moe_whole, member_index * piece_width, piece_width, 1)
    ).astype(jnp.bfloat16)


def solution(mesh):
    in_specs = (
        P("grp", "side"),
        P("grp", ("side", "tp"), None, None),
        P("grp"),
        P(("side", "tp"), None),
        P("grp", None),
        P(),
        P("grp", None),
        P("grp", None),
        P(("side", "grp", "tp"), None, None),
        P(("side", "grp", "tp"), None, None),
    )
    out_specs = P("grp", ("side", "tp"))
    return jax.shard_map(body, mesh=mesh, in_specs=in_specs, out_specs=out_specs, check_vma=False)
```

profile of v0, /device:TPU:1, one launch (start us, length us, event | category | flops | bytes accessed | tf_op | source)
XLA Modules:
  0.0 333.3 jit_solution(7118665528007655057)
XLA Ops:
  6.5 0.0 copy-start
  6.5 0.0 copy-start.3
  6.5 0.0 all-reduce.3.cloned.1.call-start
  6.6 1.0 dynamic-slice_bitcast_fusion
  7.5 0.7 broadcast_compare_fusion
  8.3 0.0 copy-start.1
  8.3 2.1 fusion.47
  10.3 2.5 collective-permute-start
  12.8 0.8 fusion.34
  13.6 0.3 collective-permute-done
  13.9 3.4 %collective-permute-start.1 = (f32[24,8]{1,0:T(8,128)S(1)}, f32[24,8]{1,0:T(8,128)S(1)}, u32[]{:S(2)}, u32[]{:S(2)}) collective-permute-start(f32[24,8]{1,0:T(8,128)S(1)} %max.6), channel_id=1, source_target_pairs={{0,2},{1,3},{2,0},{3,1},{4,6},{5,7},{6,4},{7,5},{8,10},{9,11},{10,... | collective-permute-start | bytes 2312 | tf_op jit(solution)/shard_map/ppermute | solution.py:16
  17.3 0.6 broadcast_compare_fusion.1
  17.9 0.6 collective-permute-done.1
  18.5 0.2 fusion.18
  18.7 1.0 collective-permute-start.4
  19.7 1.7 fusion.14
  21.4 0.5 collective-permute-start.2
  22.0 0.0 collective-permute-done.4
  22.0 2.9 collective-permute-start.5
  24.9 0.0 copy-done.3
  24.9 0.8 fusion.35
  25.7 0.1 copy.37
  25.8 0.1 copy.39
  25.9 1.1 collective-permute-done.5
  27.0 0.0 collective-permute-done.2
  27.0 2.0 collective-permute-start.3
  29.1 0.1 constant_dynamic-slice_fusion
  29.1 2.9 collective-permute-done.3
  32.1 0.1 fusion.37
  32.2 2.2 fusion.39
  34.4 0.0 all-reduce.3.cloned.1.call-update
  34.4 1.3 convert_multiply_fusion
  35.7 130.8 %all-reduce.3.cloned.1.call-done = f32[24,2048]{1,0:T(8,128)} async-done(((f32[24,2048]{1,0:T(8,128)}), f32[24,2048]{1,0:T(8,128)}) %all-reduce.3.cloned.1.call-update) | async-done | bytes 196624 | tf_op jit(solution)/shard_map/psum | solution.py:79
  166.5 0.0 copy-done.1
  166.5 1.1 multiply_reduce_fusion
  167.5 0.9 fusion.10
  168.5 0.1 copy.41
  168.6 13.4 %all_to_all.10 = bf16[8,1,3,2048]{3,2,1,0:T(4,128)(2,1)S(1)} all-to-all(bf16[8,1,3,2048]{3,2,1,0:T(4,128)(2,1)S(1)} %copy.41), channel_id=1, replica_groups=mesh['side'=2,'grp'=8,'tp'=8] {'grp'}, dimensions={0} | all-to-all | bytes 196608 | tf_op jit(solution)/shard_map/all_to_all | solution.py:105
  182.0 3.7 %fusion.4 = f32[8,1,3,1536]{3,0,2,1:T(8,128)S(1)} fusion(bf16[1,2048,1536]{2,1,0:T(8,128)(2,1)} %param.18, bf16[8,1,3,2048]{3,2,1,0:T(4,128)(2,1)S(1)} %all_to_all.10), kind=kOutput, calls=%fused_computation.4 | convolution fusion | flops 150994944 | bytes 6537216 | tf_op jit(solution)/shard_map/gjcd,jdf->gjcf/dot_general | solution.py:103
  185.7 0.0 copy-done
  185.7 0.0 copy-start.2
  185.7 0.5 fusion.11
  186.2 0.7 copy.43
  187.0 3.4 %all-to-all-start.1 = ((bf16[8,1,3,2048]{3,2,1,0:T(4,128)(2,1)}), bf16[8,1,3,2048]{3,2,1,0:T(4,128)(2,1)S(1)}, u32[]{:S(2)}, u32[]{:S(2)}) async-start(bf16[8,1,3,2048]{3,2,1,0:T(4,128)(2,1)} %copy.43), calls=%async_computation.1 | async-start | bytes 262144 | tf_op jit(solution)/shard_map/all_to_all | solution.py:116
  190.3 0.0 all-reduce.5.cloned.1.call-start
  190.4 0.0 copy-done.2
  190.4 6.8 %all-to-all-done.1 = bf16[8,1,3,2048]{3,2,1,0:T(4,128)(2,1)S(1)} async-done(((bf16[8,1,3,2048]{3,2,1,0:T(4,128)(2,1)}), bf16[8,1,3,2048]{3,2,1,0:T(4,128)(2,1)S(1)}, u32[]{:S(2)}, u32[]{:S(2)}) %all-to-all-start.1) | async-done | bytes 98336 | tf_op jit(solution)/shard_map/all_to_all | solution.py:116
  197.2 0.7 reshape.139
  197.9 1.9 fusion.48
  199.8 0.0 all-reduce.5.cloned.1.call-update
  199.8 125.3 %all-reduce.5.cloned.1.call-done = f32[24,2048]{1,0:T(8,128)} async-done(((f32[24,2048]{1,0:T(8,128)}), f32[24,2048]{1,0:T(8,128)}) %all-reduce.5.cloned.1.call-update) | async-done | bytes 196624 | tf_op jit(solution)/shard_map/psum | solution.py:124
  325.1 1.3 add_convert_fusion.1
  (12 shorter events, 0.1 us)
Async XLA Ops:
  6.5 179.2 %copy-start = (bf16[1,768,2048]{2,1,0:T(8,128)(2,1)S(1)}, bf16[1,768,2048]{2,1,0:T(8,128)(2,1)}, u32[]{:S(2)}) copy-start(bf16[1,768,2048]{2,1,0:T(8,128)(2,1)} %param.19) | copy-start | bytes 9437188
  6.5 18.4 %copy-start.3 = (s32[24,8]{0,1:T(8,128)S(1)}, s32[24,8]{0,1:T(8,128)}, u32[]{:S(2)}) copy-start(s32[24,8]{0,1:T(8,128)} %param.16) | copy-start | bytes 2308
  6.5 159.9 %all-reduce.3.cloned.1.call-start = ((), (), s32[]{:S(2)}) async-start(), calls=%async_computation.2 | async-start | bytes 393216 | tf_op jit(solution)/shard_map/psum | solution.py:79
  8.3 158.2 %copy-start.1 = (bf16[24,2048]{1,0:T(8,128)(2,1)S(1)}, bf16[24,2048]{1,0:T(8,128)(2,1)}, u32[]{:S(2)}) copy-start(bf16[24,2048]{1,0:T(8,128)(2,1)} %param.14) | copy-start | bytes 294916
  10.3 3.6 %collective-permute-start = (f32[24,8]{1,0:T(8,128)S(1)}, f32[24,8]{1,0:T(8,128)S(1)}, u32[]{:S(2)}, u32[]{:S(2)}) collective-permute-start(f32[24,8]{1,0:T(8,128)S(1)} %get-tuple-element.9), channel_id=1, source_target_pairs={{0,1},{1,0},{2,3},{3,2},{4,5},{5,4},{6,7},{7,6},{8,9},{9,8},{10,11... | collective-permute-start | bytes 2312 | tf_op jit(solution)/shard_map/ppermute | solution.py:16
  13.9 4.6 %collective-permute-start.1 = (f32[24,8]{1,0:T(8,128)S(1)}, f32[24,8]{1,0:T(8,128)S(1)}, u32[]{:S(2)}, u32[]{:S(2)}) collective-permute-start(f32[24,8]{1,0:T(8,128)S(1)} %max.6), channel_id=1, source_target_pairs={{0,2},{1,3},{2,0},{3,1},{4,6},{5,7},{6,4},{7,5},{8,10},{9,11},{10,... | collective-permute-start | bytes 2312 | tf_op jit(solution)/shard_map/ppermute | solution.py:16
  18.7 3.3 collective-permute-start.4
  21.4 5.6 %collective-permute-start.2 = (f32[24,8,128]{2,1,0:T(8,128)S(1)}, f32[24,8,128]{2,1,0:T(8,128)S(1)}, u32[]{:S(2)}, u32[]{:S(2)}) collective-permute-start(f32[24,8,128]{2,1,0:T(8,128)S(1)} %fusion.14), channel_id=1, source_target_pairs={{0,1},{1,0},{2,3},{3,2},{4,5},{5,4},{6,7},{7,6},{8,9},{9,8},{10,11... | collective-permute-start | bytes 294920 | tf_op jit(solution)/shard_map/ppermute | solution.py:16
  22.0 5.0 %collective-permute-start.5 = (f32[24,8]{1,0:T(8,128)S(1)}, f32[24,8]{1,0:T(8,128)S(1)}, u32[]{:S(2)}, u32[]{:S(2)}) collective-permute-start(f32[24,8]{1,0:T(8,128)S(1)} %add.92), channel_id=1, source_target_pairs={{0,2},{1,3},{2,0},{3,1},{4,6},{5,7},{6,4},{7,5},{8,10},{9,11},{10,... | collective-permute-start | bytes 2312 | tf_op jit(solution)/shard_map/ppermute | solution.py:16
  27.0 5.1 %collective-permute-start.3 = (f32[24,8,128]{2,1,0:T(8,128)S(1)}, f32[24,8,128]{2,1,0:T(8,128)S(1)}, u32[]{:S(2)}, u32[]{:S(2)}) collective-permute-start(f32[24,8,128]{2,1,0:T(8,128)S(1)} %add.90), channel_id=1, source_target_pairs={{0,2},{1,3},{2,0},{3,1},{4,6},{5,7},{6,4},{7,5},{8,10},{9,11},{10,... | collective-permute-start | bytes 294920 | tf_op jit(solution)/shard_map/ppermute | solution.py:16
  185.7 4.7 %copy-start.2 = (f32[24,8,3]{0,2,1:T(4,128)S(1)}, f32[24,8,3]{0,2,1:T(4,128)}, u32[]{:S(2)}) copy-start(f32[24,8,3]{0,2,1:T(4,128)} %get-tuple-element.7) | copy-start | bytes 6916
  187.0 10.3 %all-to-all-start.1 = ((bf16[8,1,3,2048]{3,2,1,0:T(4,128)(2,1)}), bf16[8,1,3,2048]{3,2,1,0:T(4,128)(2,1)S(1)}, u32[]{:S(2)}, u32[]{:S(2)}) async-start(bf16[8,1,3,2048]{3,2,1,0:T(4,128)(2,1)} %copy.43), calls=%async_computation.1 | async-start | bytes 262144 | tf_op jit(solution)/shard_map/all_to_all | solution.py:116
  190.3 134.8 %all-reduce.5.cloned.1.call-start = ((), (), s32[]{:S(2)}) async-start(), calls=%async_computation.3 | async-start | bytes 393216 | tf_op jit(solution)/shard_map/psum | solution.py:124
Sparse Core Ops, SparseCore 0:
  34.5 131.9 all-reduce.2
  199.9 125.1 all-reduce.4
where the time goes:
time: 334 us; the launch traced here: 333 us
  waiting for transfers between devices  268 us (80%)
  starting transfers between devices  15.9 us (5%)
  between operations  13.5 us (4%)
  blocking collectives  13.4 us (4%)
  matrix products  13 us (4%)
  other arithmetic  6.89 us (2%)
    psum x1, waiting for transfers between devices, body(): summed = lax.psum(projected, ('side', 'tp'))  131 us
    psum x1, waiting for transfers between devices, body(): moe_whole = lax.psum(moe_part, ('side', 'tp'))  125 us
    all_to_all x1, blocking collectives, body(): lax.all_to_all(outgoing, 'grp', split_axis=0, concat_axis=0, tiled=True)  13.4 us
    ppermute x6, starting transfers between devices, swapped(): return lax.ppermute(value, axis, pairs)  12.4 us
    all_to_all x1, waiting for transfers between devices, body(): lax.all_to_all(produced, 'grp', split_axis=0, concat_axis=0, tiled=True)  6.8 us
  transfers between devices with their start and end apart: 9, of which 7 were waited for; matrix products, arithmetic and copies ran while one was open for 2% of the time, Pallas kernels for 0%

commit v1 on v0

--- a/solution.py
+++ b/solution.py
@@ -76,7 +76,7 @@
         row_count, per_member * HD
     )
     projected = jnp.dot(mine, out_weight, preferred_element_type=jnp.float32)
-    summed = lax.psum(projected, ("side", "tp"))
+    summed = lax.psum(lax.psum(projected, "tp"), "side")
     middle = (resid.astype(jnp.float32) + summed).astype(jnp.bfloat16)
     middle_wide = middle.astype(jnp.float32)
     inv_rms = lax.rsqrt(jnp.mean(middle_wide * middle_wide, axis=-1, keepdims=True) + 1e-06)

time: 334 us -> 308 us (0.922)
  waiting for transfers between devices: 268 us -> 244 us
    psum x1 -> x2, waiting for transfers between devices: 131 us -> 105 us  [body(): summed = lax.psum(lax.psum(projected, 'tp'), 'side')]
  transfers between devices with their start and end apart: 9 -> 10, of which waited for: 7 -> 8; matrix products, arithmetic and copies ran while one was open for 2% -> 1% of each run, Pallas kernels for 0% -> 0%
where the time goes in v1:
time: 308 us; the launch traced here: 307 us
  waiting for transfers between devices  244 us (79%)
  starting transfers between devices  15.9 us (5%)
  blocking collectives  13.3 us (4%)
  between operations  13.2 us (4%)
  matrix products  13 us (4%)
  other arithmetic  4.98 us (2%)
    psum x1, waiting for transfers between devices, body(): moe_whole = lax.psum(moe_part, ('side', 'tp'))  126 us
    psum x2, waiting for transfers between devices, body(): summed = lax.psum(lax.psum(projected, 'tp'), 'side')  105 us
    all_to_all x1, blocking collectives, body(): lax.all_to_all(outgoing, 'grp', split_axis=0, concat_axis=0, tiled=True)  13.3 us
    ppermute x6, starting transfers between devices, swapped(): return lax.ppermute(value, axis, pairs)  12.4 us
    all_to_all x1, waiting for transfers between devices, body(): lax.all_to_all(produced, 'grp', split_axis=0, concat_axis=0, tiled=True)  6.8 us
    ppermute x6, waiting for transfers between devices, swapped(): return lax.ppermute(value, axis, pairs)  6.2 us
  transfers between devices with their start and end apart: 10, of which 8 were waited for; matrix products, arithmetic and copies ran while one was open for 1% of the time, Pallas kernels for 0%

profile of v1, /device:TPU:1, one launch (start us, length us, event | category | flops | bytes accessed | tf_op | source)
XLA Modules:
  0.0 307.0 jit_solution(18003189197908842500)
XLA Ops:
  6.5 0.0 copy-start
  6.5 0.0 copy-start.3
  6.5 0.0 all-reduce.4.cloned.1.call-start
  6.6 1.0 dynamic-slice_bitcast_fusion
  7.5 0.7 broadcast_compare_fusion
  8.3 2.1 fusion.47
  10.3 0.0 copy-start.1
  10.3 2.5 collective-permute-start
  12.8 1.1 collective-permute-done
  13.9 3.4 %collective-permute-start.1 = (f32[24,8]{1,0:T(8,128)S(1)}, f32[24,8]{1,0:T(8,128)S(1)}, u32[]{:S(2)}, u32[]{:S(2)}) collective-permute-start(f32[24,8]{1,0:T(8,128)S(1)} %max.6), channel_id=1, source_target_pairs={{0,2},{1,3},{2,0},{3,1},{4,6},{5,7},{6,4},{7,5},{8,10},{9,11},{10,... | collective-permute-start | bytes 2312 | tf_op jit(solution)/shard_map/ppermute | solution.py:16
  17.3 0.8 fusion.35
  18.1 0.4 collective-permute-done.1
  18.5 0.2 fusion.18
  18.7 1.0 collective-permute-start.4
  19.7 1.7 fusion.14
  21.4 0.5 collective-permute-start.2
  21.9 0.0 collective-permute-done.4
  22.0 2.9 collective-permute-start.5
  24.9 0.0 copy-done.3
  24.9 0.1 fusion.34
  25.0 0.1 copy.37
  25.1 0.1 copy.39
  25.2 1.8 collective-permute-done.5
  27.0 0.0 collective-permute-done.2
  27.0 2.0 collective-permute-start.3
  29.0 0.1 constant_dynamic-slice_fusion
  29.1 2.9 collective-permute-done.3
  32.1 0.1 fusion.37
  32.2 2.2 fusion.39
  34.3 0.0 all-reduce.4.cloned.1.call-update
  34.4 0.0 all-reduce.6.cloned.1.call-start
  34.4 74.9 %all-reduce.4.cloned.1.call-done = f32[24,2048]{1,0:T(8,128)} async-done(((f32[24,2048]{1,0:T(8,128)}), f32[24,2048]{1,0:T(8,128)}) %all-reduce.4.cloned.1.call-update) | async-done | bytes 196624 | tf_op jit(solution)/shard_map/psum | solution.py:79
  109.4 0.0 all-reduce.6.cloned.1.call-update
  109.4 0.6 convert_multiply_fusion
  110.0 30.4 %all-reduce.6.cloned.1.call-done = f32[24,2048]{1,0:T(8,128)} async-done(((f32[24,2048]{1,0:T(8,128)}), f32[24,2048]{1,0:T(8,128)}) %all-reduce.6.cloned.1.call-update) | async-done | bytes 196624 | tf_op jit(solution)/shard_map/psum | solution.py:79
  140.4 0.0 copy-done.1
  140.4 1.1 multiply_reduce_fusion
  141.5 0.9 fusion.10
  142.4 0.1 copy.41
  142.5 13.3 %all_to_all.10 = bf16[8,1,3,2048]{3,2,1,0:T(4,128)(2,1)S(1)} all-to-all(bf16[8,1,3,2048]{3,2,1,0:T(4,128)(2,1)S(1)} %copy.41), channel_id=1, replica_groups=mesh['side'=2,'grp'=8,'tp'=8] {'grp'}, dimensions={0} | all-to-all | bytes 196608 | tf_op jit(solution)/shard_map/all_to_all | solution.py:105
  155.8 3.7 %fusion.4 = f32[8,1,3,1536]{3,0,2,1:T(8,128)S(1)} fusion(bf16[1,2048,1536]{2,1,0:T(8,128)(2,1)} %param.18, bf16[8,1,3,2048]{3,2,1,0:T(4,128)(2,1)S(1)} %all_to_all.10), kind=kOutput, calls=%fused_computation.4 | convolution fusion | flops 150994944 | bytes 6537216 | tf_op jit(solution)/shard_map/gjcd,jdf->gjcf/dot_general | solution.py:103
  159.5 0.0 copy-done
  159.5 0.0 copy-start.2
  159.6 0.5 fusion.11
  160.1 0.7 copy.43
  160.8 3.4 %all-to-all-start.1 = ((bf16[8,1,3,2048]{3,2,1,0:T(4,128)(2,1)}), bf16[8,1,3,2048]{3,2,1,0:T(4,128)(2,1)S(1)}, u32[]{:S(2)}, u32[]{:S(2)}) async-start(bf16[8,1,3,2048]{3,2,1,0:T(4,128)(2,1)} %copy.43), calls=%async_computation.1 | async-start | bytes 262144 | tf_op jit(solution)/shard_map/all_to_all | solution.py:116
  164.2 0.0 all-reduce.8.cloned.1.call-start
  164.2 0.0 copy-done.2
  164.3 6.8 %all-to-all-done.1 = bf16[8,1,3,2048]{3,2,1,0:T(4,128)(2,1)S(1)} async-done(((bf16[8,1,3,2048]{3,2,1,0:T(4,128)(2,1)}), bf16[8,1,3,2048]{3,2,1,0:T(4,128)(2,1)S(1)}, u32[]{:S(2)}, u32[]{:S(2)}) %all-to-all-start.1) | async-done | bytes 98336 | tf_op jit(solution)/shard_map/all_to_all | solution.py:116
  171.1 0.7 reshape.139
  171.8 1.9 fusion.48
  173.6 0.0 all-reduce.8.cloned.1.call-update
  173.7 125.5 %all-reduce.8.cloned.1.call-done = f32[24,2048]{1,0:T(8,128)} async-done(((f32[24,2048]{1,0:T(8,128)}), f32[24,2048]{1,0:T(8,128)}) %all-reduce.8.cloned.1.call-update) | async-done | bytes 196624 | tf_op jit(solution)/shard_map/psum | solution.py:124
  299.2 1.3 add_convert_fusion.1
  (13 shorter events, 0.1 us)
Async XLA Ops:
  6.5 153.0 %copy-start = (bf16[1,768,2048]{2,1,0:T(8,128)(2,1)S(1)}, bf16[1,768,2048]{2,1,0:T(8,128)(2,1)}, u32[]{:S(2)}) copy-start(bf16[1,768,2048]{2,1,0:T(8,128)(2,1)} %param.19) | copy-start | bytes 9437188
  6.5 18.4 %copy-start.3 = (s32[24,8]{0,1:T(8,128)S(1)}, s32[24,8]{0,1:T(8,128)}, u32[]{:S(2)}) copy-start(s32[24,8]{0,1:T(8,128)} %param.16) | copy-start | bytes 2308
  6.5 102.8 %all-reduce.4.cloned.1.call-start = ((), (), s32[]{:S(2)}) async-start(), calls=%async_computation.2 | async-start | bytes 393216 | tf_op jit(solution)/shard_map/psum | solution.py:79
  10.3 130.1 %copy-start.1 = (bf16[24,2048]{1,0:T(8,128)(2,1)S(1)}, bf16[24,2048]{1,0:T(8,128)(2,1)}, u32[]{:S(2)}) copy-start(bf16[24,2048]{1,0:T(8,128)(2,1)} %param.14) | copy-start | bytes 294916
  10.3 3.6 %collective-permute-start = (f32[24,8]{1,0:T(8,128)S(1)}, f32[24,8]{1,0:T(8,128)S(1)}, u32[]{:S(2)}, u32[]{:S(2)}) collective-permute-start(f32[24,8]{1,0:T(8,128)S(1)} %get-tuple-element.9), channel_id=1, source_target_pairs={{0,1},{1,0},{2,3},{3,2},{4,5},{5,4},{6,7},{7,6},{8,9},{9,8},{10,11... | collective-permute-start | bytes 2312 | tf_op jit(solution)/shard_map/ppermute | solution.py:16
  13.9 4.6 %collective-permute-start.1 = (f32[24,8]{1,0:T(8,128)S(1)}, f32[24,8]{1,0:T(8,128)S(1)}, u32[]{:S(2)}, u32[]{:S(2)}) collective-permute-start(f32[24,8]{1,0:T(8,128)S(1)} %max.6), channel_id=1, source_target_pairs={{0,2},{1,3},{2,0},{3,1},{4,6},{5,7},{6,4},{7,5},{8,10},{9,11},{10,... | collective-permute-start | bytes 2312 | tf_op jit(solution)/shard_map/ppermute | solution.py:16
  18.7 3.3 %collective-permute-start.4 = (f32[24,8]{1,0:T(8,128)S(1)}, f32[24,8]{1,0:T(8,128)S(1)}, u32[]{:S(2)}, u32[]{:S(2)}) collective-permute-start(f32[24,8]{1,0:T(8,128)S(1)} %fusion.18), channel_id=1, source_target_pairs={{0,1},{1,0},{2,3},{3,2},{4,5},{5,4},{6,7},{7,6},{8,9},{9,8},{10,11... | collective-permute-start | bytes 2312 | tf_op jit(solution)/shard_map/ppermute | solution.py:16
  21.4 5.6 %collective-permute-start.2 = (f32[24,8,128]{2,1,0:T(8,128)S(1)}, f32[24,8,128]{2,1,0:T(8,128)S(1)}, u32[]{:S(2)}, u32[]{:S(2)}) collective-permute-start(f32[24,8,128]{2,1,0:T(8,128)S(1)} %fusion.14), channel_id=1, source_target_pairs={{0,1},{1,0},{2,3},{3,2},{4,5},{5,4},{6,7},{7,6},{8,9},{9,8},{10,11... | collective-permute-start | bytes 294920 | tf_op jit(solution)/shard_map/ppermute | solution.py:16
  22.0 5.0 %collective-permute-start.5 = (f32[24,8]{1,0:T(8,128)S(1)}, f32[24,8]{1,0:T(8,128)S(1)}, u32[]{:S(2)}, u32[]{:S(2)}) collective-permute-start(f32[24,8]{1,0:T(8,128)S(1)} %add.94), channel_id=1, source_target_pairs={{0,2},{1,3},{2,0},{3,1},{4,6},{5,7},{6,4},{7,5},{8,10},{9,11},{10,... | collective-permute-start | bytes 2312 | tf_op jit(solution)/shard_map/ppermute | solution.py:16
  27.0 5.1 %collective-permute-start.3 = (f32[24,8,128]{2,1,0:T(8,128)S(1)}, f32[24,8,128]{2,1,0:T(8,128)S(1)}, u32[]{:S(2)}, u32[]{:S(2)}) collective-permute-start(f32[24,8,128]{2,1,0:T(8,128)S(1)} %add.92), channel_id=1, source_target_pairs={{0,2},{1,3},{2,0},{3,1},{4,6},{5,7},{6,4},{7,5},{8,10},{9,11},{10,... | collective-permute-start | bytes 294920 | tf_op jit(solution)/shard_map/ppermute | solution.py:16
  34.4 106.1 %all-reduce.6.cloned.1.call-start = ((), (), s32[]{:S(2)}) async-start(), calls=%async_computation.3 | async-start | bytes 393216 | tf_op jit(solution)/shard_map/psum | solution.py:79
  159.5 4.7 %copy-start.2 = (f32[24,8,3]{0,2,1:T(4,128)S(1)}, f32[24,8,3]{0,2,1:T(4,128)}, u32[]{:S(2)}) copy-start(f32[24,8,3]{0,2,1:T(4,128)} %get-tuple-element.7) | copy-start | bytes 6916
  160.8 10.2 %all-to-all-start.1 = ((bf16[8,1,3,2048]{3,2,1,0:T(4,128)(2,1)}), bf16[8,1,3,2048]{3,2,1,0:T(4,128)(2,1)S(1)}, u32[]{:S(2)}, u32[]{:S(2)}) async-start(bf16[8,1,3,2048]{3,2,1,0:T(4,128)(2,1)} %copy.43), calls=%async_computation.1 | async-start | bytes 262144 | tf_op jit(solution)/shard_map/all_to_all | solution.py:116
  164.2 135.0 %all-reduce.8.cloned.1.call-start = ((), (), s32[]{:S(2)}) async-start(), calls=%async_computation.4 | async-start | bytes 393216 | tf_op jit(solution)/shard_map/psum | solution.py:124
Sparse Core Ops, SparseCore 0:
  34.5 74.8 all-reduce.3
  111.9 28.4 all-reduce.5
  173.8 125.3 all-reduce.7
